TPU v7x, 128 devices: a whole 4x4x4 slice. The times are simulated.
128 devices in a mesh: row: 8 (over z_hi, x), blk: 16 (over z_lo, y, core).
Axes of the slice: x: 4, y: 4, z: 4 (z_hi: 2, z_lo: 2; z = z_hi * 2 + z_lo), core: 2. Of those that a mesh axis runs over, the one named last changes fastest.
Arguments:
- spike_counts: int32 [16384, 2048], P(('row', 'blk')), may hold values from 0 to 23, as said below
- kernel_taps: int32 [16], replicated, may hold values from 1 to 8
- lag_bins: int32 [2], replicated, may hold values from 1 to 32, as said below
Outputs:
- correlogram: bfloat16 [2, 16384, 8, 2048], P(None, 'row', None, 'blk')
Inputs may be any that keep to these rules, and one draw needn't show every extreme that they name: `spike_counts`: neurons fire at different rates and share a common drive. `lag_bins`: the second lag equals 32; the first lies between 1 and 31.
All inputs are finite; a program needn't handle non-finite values.
Results may differ from a plain program's by a relative error of at most 0.0034.
Values may be sent and summed in bfloat16 or wider, within the bound.
A program may use at most 128 MiB of HBM per device.

v0:
```python
import jax
import jax.numpy as jnp
from jax import lax
from jax.sharding import PartitionSpec as P

NEURONS = 16384
BINS = 2048
TAPS = 16


def smoothed(spike_counts, kernel_taps):
    counts = spike_counts.astype(jnp.float32)
    weights = kernel_taps.astype(jnp.float32) / jnp.sum(kernel_taps.astype(jnp.float32))
    padded = jnp.pad(counts, ((0, 0), (TAPS - 1, 0)))
    result = jnp.zeros_like(counts)
    for delay in range(TAPS):
        result = result + weights[delay] * padded[:, TAPS - 1 - delay : TAPS - 1 - delay + BINS]
    return result


def later_bins(data, lag):
    padded = jnp.pad(data, ((0, 0), (0, BINS)))
    return lax.dynamic_slice_in_dim(padded, lag, BINS, 1)


def shards(spike_counts, kernel_taps, lag_bins):
    smooth = smoothed(spike_counts, kernel_taps)
    centred = smooth - jnp.mean(smooth, axis=1, keepdims=True)
    totals = lax.psum(jnp.sum(centred, axis=0), ("row", "blk"))
    residual_part = centred - (totals / NEURONS)[None, :]
    zscored = (
        residual_part
        * lax.rsqrt(jnp.mean(residual_part * residual_part, axis=1, keepdims=True) + 1e-05)
    ).astype(jnp.bfloat16)
    span_rows = zscored.shape[0]
    groups = lax.axis_size("row")
    columns = lax.all_gather(zscored, "row", axis=0, tiled=True)
    stacked = jnp.concatenate(
        [later_bins(columns, lag_bins[0]), later_bins(columns, lag_bins[1])], axis=0
    )
    piece = lax.all_gather(zscored, "blk", axis=0, tiled=True)
    product = jnp.dot(piece, stacked.T, preferred_element_type=jnp.float32) / BINS
    product = product.reshape(piece.shape[0], 2, groups, span_rows)
    return jnp.transpose(product, (1, 0, 2, 3)).astype(jnp.bfloat16)


def solution(mesh):
    placed = (P(("row", "blk"), None), P(), P())
    return jax.shard_map(
        shards, mesh=mesh, in_specs=placed, out_specs=P(None, "row", None, "blk"), check_vma=False
    )
```

profile of v0, /device:TPU:1, one launch (start us, length us, event | category | flops | bytes accessed | tf_op | source)
XLA Modules:
  0.0 258.9 jit_solution(15566849793997691235)
XLA Ops:
  6.5 0.0 copy-start
  6.5 0.0 all-gather.5.cloned.1.call-start
  6.5 1.3 convert_reduce_fusion
  7.8 1.3 convert_divide_fusion
  9.1 0.7 fusion.8
  9.8 1.3 convert_element_type.25
  11.2 14.1 %fusion.6 = (f32[128]{0:T(128)S(1)}, f32[128,2048]{1,0:T(8,128)S(1)}) fusion(f32[]{:T(128)} %bitcast.15, f32[]{:T(128)} %bitcast.14, f32[]{:T(128)} %bitcast.13, f32[]{:T(128)} %bitcast.12, f32[]{:T(128)} %bitcast.11, f32[]{:T(128)} %bitcast.10, f32[]{:T(128)} %bitcast.9, f32[]{:T(128)} %bitcast.8, f32[]{:T(128)} %bitcast.7, f32[]{:T(128)} %bitcast.6, ...), kind=kLoop, calls=%fused_computation.19 | loop fusion | flops 8388480 | bytes 2097728 | tf_op jit(solution)/shard_map/reduce_sum | solution.py:28
  25.3 0.2 subtract_reduce_fusion
  25.5 68.7 %psum.7 = f32[2048]{0:T(1024)S(1)} all-reduce(f32[2048]{0:T(1024)S(1)} %subtract_reduce_fusion), channel_id=1, replica_groups=mesh['row'=8,'blk'=16] {'row','blk'}, use_global_device_ids=true, to_apply=%region_3.4 | all-reduce | flops 2048 | bytes 16384 | tf_op jit(solution)/shard_map/psum | solution.py:29
  94.2 0.3 multiply_reduce_fusion
  94.5 1.0 multiply_convert_fusion.1
  95.5 0.0 all-gather.5.cloned.1.call-update
  95.6 0.2 all-gather.3.cloned.1.call-start
  95.8 0.5 all-gather.3.cloned.1.call-update
  96.3 0.0 copy-done
  96.3 0.6 fusion.7
  100.7 62.5 %all-gather.5.cloned.1.call-done = bf16[1024,2048]{1,0:T(8,128)(2,1)} async-done(((bf16[128,2048]{1,0:T(8,128)(2,1)}), bf16[1024,2048]{1,0:T(8,128)(2,1)}) %all-gather.5.cloned.1.call-update) | async-done | bytes 4194320 | tf_op jit(solution)/shard_map/all_gather | solution.py:37
  163.2 10.0 %pad_dynamic-slice_fusion.1 = (bf16[1024,2048]{1,0:T(8,128)(2,1)}, bf16[1024,2048]{1,0:T(8,128)(2,1)}) fusion(s32[]{:T(128)S(6)} %select_n.6, bf16[1024,2048]{1,0:T(8,128)(2,1)} %all-gather.5.cloned.1.call-done, s32[]{:T(128)S(6)} %select_n.7), kind=kLoop, calls=%fused_computation.2 | loop fusion | bytes 12582920 | tf_op jit(solution)/shard_map/dynamic_slice | solution.py:23
  173.2 42.5 %all-gather.3.cloned.1.call-done = bf16[2048,2048]{1,0:T(8,128)(2,1)} async-done(((bf16[128,2048]{1,0:T(8,128)(2,1)}), bf16[2048,2048]{1,0:T(8,128)(2,1)}) %all-gather.3.cloned.1.call-update) | async-done | bytes 8388624 | tf_op jit(solution)/shard_map/all_gather | solution.py:41
  215.7 23.8 %multiply_convert_fusion = bf16[2048,2048]{0,1:T(8,128)(2,1)} fusion(bf16[2048,2048]{1,0:T(8,128)(2,1)} %all-gather.3.cloned.1.call-done, bf16[1024,2048]{1,0:T(8,128)(2,1)} %get-tuple-element.8, bf16[1024,2048]{1,0:T(8,128)(2,1)} %get-tuple-element.7), kind=kOutput, calls=%fused_computation | convolution fusion | flops 17205035008 | bytes 25165824 | tf_op jit(solution)/shard_map/dot_general | solution.py:42
  239.5 12.6 %copy.4 = bf16[2048,2,8,128]{3,2,0,1:T(8,128)(2,1)} copy(bf16[2048,2,8,128]{0,3,2,1:T(8,128)(2,1)} %bitcast.21) | data formatting | bytes 16777216 | tf_op jit(solution)/shard_map/convert_element_type | solution.py:44
  (3 shorter events, 0.0 us)
Async XLA Ops:
  6.5 89.8 %copy-start = (s32[2]{0:T(128)S(1)}, s32[2]{0:T(128)}, u32[]{:S(2)}) copy-start(s32[2]{0:T(128)} %param.5) | copy-start | bytes 28
  6.5 156.7 %all-gather.5.cloned.1.call-start = ((), (), s32[]{:S(2)}) async-start(), calls=%async_computation.1 | async-start | bytes 4718592 | tf_op jit(solution)/shard_map/all_gather | solution.py:37
  95.6 120.2 %all-gather.3.cloned.1.call-start = ((), (), s32[]{:S(2)}) async-start(), calls=%async_computation | async-start | bytes 8912896 | tf_op jit(solution)/shard_map/all_gather | solution.py:41
Sparse Core Ops, SparseCore 0:
  95.7 67.5 all-gather.4
  165.0 50.7 all-gather.2
where the time goes:
time: 260 us; the launch traced here: 259 us
  waiting for transfers between devices  106 us (41%)
  blocking collectives  68.7 us (26%)
  local copies, waits for them, and re-layouts  23.9 us (9%)
  matrix products  23.8 us (9%)
  other arithmetic  19.5 us (8%)
  between operations  17.2 us (7%)
    psum x1, blocking collectives, shards(): totals = lax.psum(jnp.sum(centred, axis=0), ('row', 'blk'))  68.7 us
    all_gather x1, waiting for transfers between devices, shards(): columns = lax.all_gather(zscored, 'row', axis=0, tiled=True)  62.5 us
    all_gather x1, waiting for transfers between devices, shards(): piece = lax.all_gather(zscored, 'blk', axis=0, tiled=True)  42.5 us
    dot_general x1, matrix products, shards(): jnp.dot(piece, stacked.T, preferred_element_type=jnp.float32) / BINS  23.8 us
    reduce_sum x1, other arithmetic, shards(): centred = smooth - jnp.mean(smooth, axis=1, keepdims=True)  14.1 us
    convert_element_type x1, local copies, waits for them, and re-layouts, shards(): return jnp.transpose(product, (1, 0, 2, 3)).astype(jnp.bfloat16)  12.6 us
    dynamic_slice x1, local copies, waits for them, and re-layouts, later_bins(): return lax.dynamic_slice_in_dim(padded, lag, BINS, 1)  9.97 us
  transfers between devices with their start and end apart: 2, of which 2 were waited for; matrix products, arithmetic and copies ran while one was open for 4% of the time, Pallas kernels for 0%

commit v1 on v0

--- a/solution.py
+++ b/solution.py
@@ -34,7 +34,10 @@
     ).astype(jnp.bfloat16)
     span_rows = zscored.shape[0]
     groups = lax.axis_size("row")
-    columns = lax.all_gather(zscored, "row", axis=0, tiled=True)
+    n_dev = lax.axis_size("row")
+    blocks = jnp.stack([zscored for _ in range(n_dev)])
+    blocks = lax.all_to_all(blocks, "row", split_axis=0, concat_axis=0)
+    columns = jnp.concatenate(blocks, axis=0)
     stacked = jnp.concatenate(
         [later_bins(columns, lag_bins[0]), later_bins(columns, lag_bins[1])], axis=0
     )

time: 260 us -> 234 us (0.900)
  waiting for transfers between devices: 106 us -> 71.5 us
  starting transfers between devices: 0.22 us -> 4.84 us
  local copies, waits for them, and re-layouts: 23.9 us -> 27.4 us
    all_gather x1 -> x0, waiting for transfers between devices: 62.5 us -> none  [shards(): columns = lax.all_gather(zscored, 'row', axis=0, tiled=True)]
    all_to_all x0 -> x1, waiting for transfers between devices: none -> 55.8 us  [shards(): blocks = lax.all_to_all(blocks, 'row', split_axis=0, concat_axis=0)]
    all_gather x1, waiting for transfers between devices: 42.5 us -> 15.7 us  [shards(): piece = lax.all_gather(zscored, 'blk', axis=0, tiled=True)]
    all_to_all x0 -> x1, starting transfers between devices: none -> 4.83 us  [shards(): blocks = lax.all_to_all(blocks, 'row', split_axis=0, concat_axis=0)]
    another operation x0 -> x1, local copies, waits for them, and re-layouts: none -> 3.58 us  [shards(): blocks = jnp.stack([zscored for _ in range(n_dev)])]
  transfers between devices with their start and end apart: 2 -> 2, of which waited for: 2 -> 2; matrix products, arithmetic and copies ran while one was open for 4% -> 6% of each run, Pallas kernels for 0% -> 0%
where the time goes in v1:
time: 234 us; the launch traced here: 233 us
  waiting for transfers between devices  71.5 us (31%)
  blocking collectives  68.7 us (29%)
  local copies, waits for them, and re-layouts  27.4 us (12%)
  matrix products  23.8 us (10%)
  other arithmetic  19.5 us (8%)
  between operations  17 us (7%)
  starting transfers between devices  4.84 us (2%)
    psum x1, blocking collectives, shards(): totals = lax.psum(jnp.sum(centred, axis=0), ('row', 'blk'))  68.7 us
    all_to_all x1, waiting for transfers between devices, shards(): blocks = lax.all_to_all(blocks, 'row', split_axis=0, concat_axis=0)  55.8 us
    dot_general x1, matrix products, shards(): jnp.dot(piece, stacked.T, preferred_element_type=jnp.float32) / BINS  23.8 us
    all_gather x1, waiting for transfers between devices, shards(): piece = lax.all_gather(zscored, 'blk', axis=0, tiled=True)  15.7 us
    reduce_sum x1, other arithmetic, shards(): centred = smooth - jnp.mean(smooth, axis=1, keepdims=True)  14.1 us
    convert_element_type x1, local copies, waits for them, and re-layouts, shards(): return jnp.transpose(product, (1, 0, 2, 3)).astype(jnp.bfloat16)  12.6 us
    dynamic_slice x1, local copies, waits for them, and re-layouts, later_bins(): return lax.dynamic_slice_in_dim(padded, lag, BINS, 1)  9.97 us
    all_to_all x1, starting transfers between devices, shards(): blocks = lax.all_to_all(blocks, 'row', split_axis=0, concat_axis=0)  4.83 us
  transfers between devices with their start and end apart: 2, of which 2 were waited for; matrix products, arithmetic and copies ran while one was open for 6% of the time, Pallas kernels for 0%

profile of v1, /device:TPU:1, one launch (start us, length us, event | category | flops | bytes accessed | tf_op | source)
XLA Modules:
  0.0 232.8 jit_solution(14180848419307631503)
XLA Ops:
  6.5 0.0 all-gather.2.cloned.1.call-start
  6.5 1.3 convert_reduce_fusion
  7.8 1.3 convert_divide_fusion
  9.1 0.7 fusion.8
  9.8 1.3 convert_element_type.25
  11.1 14.1 %fusion.6 = (f32[128]{0:T(128)S(1)}, f32[128,2048]{1,0:T(8,128)S(1)}) fusion(f32[]{:T(128)} %bitcast.15, f32[]{:T(128)} %bitcast.14, f32[]{:T(128)} %bitcast.13, f32[]{:T(128)} %bitcast.12, f32[]{:T(128)} %bitcast.11, f32[]{:T(128)} %bitcast.10, f32[]{:T(128)} %bitcast.9, f32[]{:T(128)} %bitcast.8, f32[]{:T(128)} %bitcast.7, f32[]{:T(128)} %bitcast.6, ...), kind=kLoop, calls=%fused_computation.19 | loop fusion | flops 8388480 | bytes 2097728 | tf_op jit(solution)/shard_map/reduce_sum | solution.py:28
  25.3 0.2 subtract_reduce_fusion
  25.4 0.0 copy-start
  25.5 68.7 %psum.7 = f32[2048]{0:T(1024)S(1)} all-reduce(f32[2048]{0:T(1024)S(1)} %subtract_reduce_fusion), channel_id=1, replica_groups=mesh['row'=8,'blk'=16] {'row','blk'}, use_global_device_ids=true, to_apply=%region_3.4 | all-reduce | flops 2048 | bytes 16384 | tf_op jit(solution)/shard_map/psum | solution.py:29
  94.2 0.3 multiply_reduce_fusion
  94.5 1.0 multiply_convert_fusion.1
  95.5 0.0 all-gather.2.cloned.1.call-update
  95.6 3.6 %stack.2 = bf16[8,128,2048]{2,1,0:T(8,128)(2,1)} broadcast(bf16[128,2048]{1,0:T(8,128)(2,1)} %multiply_convert_fusion.1), dimensions={1,2} | broadcast | bytes 4718592 | tf_op jit(solution)/shard_map/stack | solution.py:38
  99.1 4.8 %all-to-all-start = ((bf16[8,128,2048]{2,1,0:T(8,128)(2,1)}), bf16[8,128,2048]{2,1,0:T(8,128)(2,1)}, u32[]{:S(2)}, u32[]{:S(2)}) async-start(bf16[8,128,2048]{2,1,0:T(8,128)(2,1)} %stack.2), calls=%async_computation | async-start | bytes 8388608 | tf_op jit(solution)/shard_map/all_to_all | solution.py:39
  104.0 0.0 copy-done
  104.0 0.6 fusion.7
  108.1 55.8 %all-to-all-done = bf16[8,128,2048]{2,1,0:T(8,128)(2,1)} async-done(((bf16[8,128,2048]{2,1,0:T(8,128)(2,1)}), bf16[8,128,2048]{2,1,0:T(8,128)(2,1)}, u32[]{:S(2)}, u32[]{:S(2)}) %all-to-all-start) | async-done | bytes 4194336 | tf_op jit(solution)/shard_map/all_to_all | solution.py:39
  163.9 10.0 %pad_dynamic-slice_fusion.1 = (bf16[1024,2048]{1,0:T(8,128)(2,1)}, bf16[1024,2048]{1,0:T(8,128)(2,1)}) fusion(s32[]{:T(128)S(6)} %select_n.6, bf16[1024,2048]{1,0:T(8,128)(2,1)} %bitcast.16, s32[]{:T(128)S(6)} %select_n.7), kind=kLoop, calls=%fused_computation.2 | loop fusion | bytes 12582920 | tf_op jit(solution)/shard_map/dynamic_slice | solution.py:23
  173.9 15.7 %all-gather.2.cloned.1.call-done = bf16[2048,2048]{1,0:T(8,128)(2,1)} async-done(((bf16[128,2048]{1,0:T(8,128)(2,1)}), bf16[2048,2048]{1,0:T(8,128)(2,1)}) %all-gather.2.cloned.1.call-update) | async-done | bytes 8388624 | tf_op jit(solution)/shard_map/all_gather | solution.py:44
  189.6 23.8 %multiply_convert_fusion = bf16[2048,2048]{0,1:T(8,128)(2,1)} fusion(bf16[2048,2048]{1,0:T(8,128)(2,1)} %all-gather.2.cloned.1.call-done, bf16[1024,2048]{1,0:T(8,128)(2,1)} %get-tuple-element.8, bf16[1024,2048]{1,0:T(8,128)(2,1)} %get-tuple-element.7), kind=kOutput, calls=%fused_computation | convolution fusion | flops 17205035008 | bytes 25165824 | tf_op jit(solution)/shard_map/dot_general | solution.py:45
  213.4 12.6 %copy.4 = bf16[2048,2,8,128]{3,2,0,1:T(8,128)(2,1)} copy(bf16[2048,2,8,128]{0,3,2,1:T(8,128)(2,1)} %bitcast.22) | data formatting | bytes 16777216 | tf_op jit(solution)/shard_map/convert_element_type | solution.py:47
  (3 shorter events, 0.0 us)
Async XLA Ops:
  6.5 183.1 %all-gather.2.cloned.1.call-start = ((), (), s32[]{:S(2)}) async-start(), calls=%async_computation.1 | async-start | bytes 8912896 | tf_op jit(solution)/shard_map/all_gather | solution.py:44
  25.4 78.5 %copy-start = (s32[2]{0:T(128)S(1)}, s32[2]{0:T(128)}, u32[]{:S(2)}) copy-start(s32[2]{0:T(128)} %param.5) | copy-start | bytes 28
  99.1 64.8 %all-to-all-start = ((bf16[8,128,2048]{2,1,0:T(8,128)(2,1)}), bf16[8,128,2048]{2,1,0:T(8,128)(2,1)}, u32[]{:S(2)}, u32[]{:S(2)}) async-start(bf16[8,128,2048]{2,1,0:T(8,128)(2,1)} %stack.2), calls=%async_computation | async-start | bytes 8388608 | tf_op jit(solution)/shard_map/all_to_all | solution.py:39
Sparse Core Ops, SparseCore 0:
  95.7 93.8 all-gather.1
